TPU v7x, 512 devices: a whole 4x4x16 slice. The times are simulated.
512 devices in a mesh: dp: 8 (over y, core), station: 64 (over x, z).
Axes of the slice: x: 4, y: 4, z: 16, core: 2. Of those that a mesh axis runs over, the one named last changes fastest.
Arguments:
- query_states: bfloat16 [8, 64, 128, 768], P('dp', 'station'), may hold values from -6 to 6
- key_states: bfloat16 [8, 64, 128, 768], P('dp', 'station'), may hold values from -6 to 6
- value_states: bfloat16 [8, 64, 128, 768], P('dp', 'station'), may hold values from -15 to 15
- grad_output: bfloat16 [8, 64, 128, 768], P('dp', 'station'), may hold values from -6 to 6
- out_weight: bfloat16 [768, 768], replicated, may hold values from -0.21875 to 0.21875
- partner_ids: int32 [64, 6], replicated, may hold values from 0 to 63, as said below
- partner_count: int32 [64], replicated, may hold values from 1 to 6, as said below
Outputs:
- layer_output: bfloat16 [8, 64, 128, 768], P('dp', 'station')
- grad_query: bfloat16 [8, 64, 128, 768], P('dp', 'station')
- grad_key: bfloat16 [8, 64, 128, 768], P('dp', 'station')
- grad_value: bfloat16 [8, 64, 128, 768], P('dp', 'station')
- grad_weight: float32 [768, 768], P('dp')
Inputs may be any that keep to these rules, and one draw needn't show every extreme that they name: `partner_ids`: row s lists 6 different stations other than s, all held by devices within 3 places of the device of s along the station axis, taken as a loop (station s lies on device s); only the first partner_count[s] entries are partners. `partner_count`: some station has exactly 6 partners.
All inputs are finite; a program needn't handle non-finite values.
Results may differ from a plain program's by a relative error of at most 0.025.
Values may be sent and summed in bfloat16 or wider, within the bound.
A program may use at most 64 MiB of HBM per device.

v0:
```python
import math
import jax
import jax.numpy as jnp
from jax import lax
from jax.sharding import PartitionSpec as P

HEADS = 12
PMAX = 6
HOPS = 3
neg_big = -1e30


def from_behind(value, axis, steps):
    count = lax.axis_size(axis)
    pairs = [(source, (source + steps) % count) for source in range(count)]
    return lax.ppermute(value, axis, pairs)


def split_heads(rows_in, head_count):
    return rows_in.reshape(rows_in.shape[:-1] + (head_count, rows_in.shape[-1] // head_count))


def local(
    query_states, key_states, value_states, grad_output, out_weight, partner_ids, partner_count
):
    window_count, per_device, span_rows, model_width = query_states.shape
    head_count = HEADS
    head_width = model_width // head_count
    score_scale = 1.0 / math.sqrt(head_width)
    slot_count = PMAX + 1
    device_count = lax.axis_size("station")
    station_count = per_device * device_count
    device_no = lax.axis_index("station")
    candidates = (2 * HOPS + 1) * per_device
    first_station = (device_no - HOPS) * per_device
    key_value = jnp.stack([key_states, value_states], 0)
    pieces = []
    for offset in range(-HOPS, HOPS + 1):
        if offset == 0:
            pieces.append(key_value)
        else:
            pieces.append(from_behind(key_value, "station", -offset))
    window = jnp.concatenate(pieces, 2)
    my_partners = lax.dynamic_slice_in_dim(partner_ids, device_no * per_device, per_device, 0)
    my_counts = lax.dynamic_slice_in_dim(partner_count, device_no * per_device, per_device, 0)
    partner_pos = jnp.mod(my_partners - first_station, station_count)
    self_pos = HOPS * per_device + jnp.arange(per_device, dtype=jnp.int32)
    slot_station = jnp.concatenate([self_pos[:, None], partner_pos], 1)
    slot_live = jnp.arange(slot_count, dtype=jnp.int32)[None, :] <= my_counts[:, None]
    row_count = window_count * per_device * span_rows
    flat_grad = grad_output.reshape(row_count, model_width)
    grad_mixed = lax.dot_general(
        flat_grad, out_weight, (((1,), (1,)), ((), ())), preferred_element_type=jnp.float32
    ).astype(jnp.bfloat16)
    grad_mixed = grad_mixed.reshape(query_states.shape)

    def one_station(number):
        window_no = number // per_device
        station_no = number % per_device
        query_rows = split_heads(query_states[window_no, station_no], head_count)
        grad_rows = split_heads(grad_mixed[window_no, station_no], head_count)
        picked = jnp.take(window[:, window_no], slot_station[station_no], axis=1)
        key_rows = picked[0].reshape(slot_count * span_rows, head_count, head_width)
        value_rows = picked[1].reshape(slot_count * span_rows, head_count, head_width)
        allowed = jnp.repeat(slot_live[station_no].astype(jnp.float32), span_rows)
        scores = (
            jnp.einsum("qhd,khd->hqk", query_rows, key_rows, preferred_element_type=jnp.float32)
            * score_scale
        )
        masked = jnp.where(allowed[None, None, :] > 0, scores, neg_big)
        row_max = jnp.max(masked, -1)
        weights_raw = jnp.exp(masked - row_max[..., None])
        row_sum = jnp.sum(weights_raw, -1)
        attn_probs = weights_raw / row_sum[..., None]
        probs_half = attn_probs.astype(jnp.bfloat16)
        mixed_rows = jnp.einsum(
            "hqk,khd->qhd", probs_half, value_rows, preferred_element_type=jnp.float32
        ).astype(jnp.bfloat16)
        row_delta = jnp.sum(grad_rows.astype(jnp.float32) * mixed_rows.astype(jnp.float32), -1).T
        grad_probs = jnp.einsum(
            "qhd,khd->hqk", grad_rows, value_rows, preferred_element_type=jnp.float32
        )
        grad_scores = (attn_probs * (grad_probs - row_delta[..., None])).astype(jnp.bfloat16)
        query_grad = (
            score_scale
            * jnp.einsum("hqk,khd->qhd", grad_scores, key_rows, preferred_element_type=jnp.float32)
        ).astype(jnp.bfloat16)
        result = (
            mixed_rows.reshape(span_rows, model_width),
            query_grad.reshape(span_rows, model_width),
        )
        key_part = score_scale * jnp.einsum(
            "hqk,qhd->khd", grad_scores, query_rows, preferred_element_type=jnp.float32
        )
        value_part = jnp.einsum(
            "hqk,qhd->khd", probs_half, grad_rows, preferred_element_type=jnp.float32
        )
        result = result + (
            jnp.stack([key_part, value_part], 0).reshape(2, -1, span_rows, model_width),
        )
        return result

    outputs = lax.map(one_station, jnp.arange(window_count * per_device, dtype=jnp.int32))
    mixed_all = outputs[0].reshape(query_states.shape)
    grad_query = outputs[1].reshape(query_states.shape)
    contribution = outputs[2].reshape(window_count, per_device, 2, -1, span_rows, model_width)
    moved = jnp.moveaxis(contribution, 2, 0).reshape(
        2, window_count, per_device * slot_count, span_rows, model_width
    )
    flat_slots = slot_station.reshape(-1)
    spread = (
        jnp.zeros((2, window_count, candidates, span_rows, model_width), jnp.float32)
        .at[:, :, flat_slots]
        .add(moved)
    )
    own_grads = spread[:, :, HOPS * per_device : (HOPS + 1) * per_device]
    for offset in range(-HOPS, HOPS + 1):
        if offset != 0:
            lower = (offset + HOPS) * per_device
            own_grads = own_grads + from_behind(
                spread[:, :, lower : lower + per_device].astype(jnp.bfloat16), "station", offset
            ).astype(jnp.float32)
    mixed_flat = mixed_all.reshape(row_count, model_width)
    layer_output = jnp.dot(mixed_flat, out_weight, preferred_element_type=jnp.float32).astype(
        jnp.bfloat16
    )
    grad_weight = lax.psum_scatter(
        lax.dot_general(
            mixed_flat, flat_grad, (((0,), (0,)), ((), ())), preferred_element_type=jnp.float32
        ).astype(jnp.bfloat16),
        "dp",
        scatter_dimension=0,
        tiled=True,
    ).astype(jnp.float32)
    grad_weight = lax.psum(grad_weight, "station")
    grad_weight = grad_weight / math.sqrt(row_count * lax.axis_size("dp") * device_count)
    return (
        layer_output.reshape(query_states.shape),
        grad_query,
        own_grads[0].astype(jnp.bfloat16),
        own_grads[1].astype(jnp.bfloat16),
        grad_weight,
    )


def solution(mesh):
    return jax.shard_map(
        local,
        mesh=mesh,
        in_specs=(
            P("dp", "station", None, None),
            P("dp", "station", None, None),
            P("dp", "station", None, None),
            P("dp", "station", None, None),
            P(),
            P(),
            P(),
        ),
        out_specs=(
            P("dp", "station", None, None),
            P("dp", "station", None, None),
            P("dp", "station", None, None),
            P("dp", "station", None, None),
            P("dp", None),
        ),
        check_vma=False,
    )
```

profile of v0, /device:TPU:24, one launch (start us, length us, event | category | flops | bytes accessed | tf_op | source)
XLA Modules:
  0.0 522.1 jit_solution(13839279402721123467)
XLA Ops:
  8.4 6.5 %collective-permute-start = (bf16[2,1,1,128,768]{4,3,2,1,0:T(8,128)(2,1)S(1)}, bf16[2,1,1,128,768]{4,3,2,1,0:T(8,128)(2,1)}, u32[]{:S(2)}, u32[]{:S(2)}) collective-permute-start(bf16[2,1,1,128,768]{4,3,2,1,0:T(8,128)(2,1)S(1)} %pad_maximum_fusion), channel_id=1, source_target_pairs={{0,3},{1,4},{2,5},{3,6},{4,7},{5,8},{6,9},{7,10},{8,11},{9,12},{10... | collective-permute-start | bytes 1179656 | tf_op jit(solution)/shard_map/ppermute | solution.py:16
  15.0 6.4 %collective-permute-start.1 = (bf16[2,1,1,128,768]{4,3,2,1,0:T(8,128)(2,1)S(1)}, bf16[2,1,1,128,768]{4,3,2,1,0:T(8,128)(2,1)}, u32[]{:S(2)}, u32[]{:S(2)}) collective-permute-start(bf16[2,1,1,128,768]{4,3,2,1,0:T(8,128)(2,1)S(1)} %pad_maximum_fusion), channel_id=1, source_target_pairs={{0,2},{1,3},{2,4},{3,5},{4,6},{5,7},{6,8},{7,9},{8,10},{9,11},{10,... | collective-permute-start | bytes 1179656 | tf_op jit(solution)/shard_map/ppermute | solution.py:16
  21.4 3.8 collective-permute-start.2
  25.2 5.3 %collective-permute-start.3 = (bf16[2,1,1,128,768]{4,3,2,1,0:T(8,128)(2,1)S(1)}, bf16[2,1,1,128,768]{4,3,2,1,0:T(8,128)(2,1)S(1)}, u32[]{:S(2)}, u32[]{:S(2)}) collective-permute-start(bf16[2,1,1,128,768]{4,3,2,1,0:T(8,128)(2,1)S(1)} %pad_maximum_fusion), channel_id=1, source_target_pairs={{0,63},{1,0},{2,1},{3,2},{4,3},{5,4},{6,5},{7,6},{8,7},{9,8},{10,9... | collective-permute-start | bytes 1179656 | tf_op jit(solution)/shard_map/ppermute | solution.py:16
  37.4 11.0 %collective-permute-done = bf16[2,1,1,128,768]{4,3,2,1,0:T(8,128)(2,1)} collective-permute-done((bf16[2,1,1,128,768]{4,3,2,1,0:T(8,128)(2,1)S(1)}, bf16[2,1,1,128,768]{4,3,2,1,0:T(8,128)(2,1)}, u32[]{:S(2)}, u32[]{:S(2)}) %collective-permute-start) | collective-permute-done | bytes 393248 | tf_op jit(solution)/shard_map/ppermute | solution.py:16
  48.4 5.5 %collective-permute-start.5 = (bf16[2,1,1,128,768]{4,3,2,1,0:T(8,128)(2,1)S(1)}, bf16[2,1,1,128,768]{4,3,2,1,0:T(8,128)(2,1)S(1)}, u32[]{:S(2)}, u32[]{:S(2)}) collective-permute-start(bf16[2,1,1,128,768]{4,3,2,1,0:T(8,128)(2,1)S(1)} %pad_maximum_fusion), channel_id=1, source_target_pairs={{0,61},{1,62},{2,63},{3,0},{4,1},{5,2},{6,3},{7,4},{8,5},{9,6},{10... | collective-permute-start | bytes 1179656 | tf_op jit(solution)/shard_map/ppermute | solution.py:16
  55.7 8.0 %collective-permute-done.1 = bf16[2,1,1,128,768]{4,3,2,1,0:T(8,128)(2,1)} collective-permute-done((bf16[2,1,1,128,768]{4,3,2,1,0:T(8,128)(2,1)S(1)}, bf16[2,1,1,128,768]{4,3,2,1,0:T(8,128)(2,1)}, u32[]{:S(2)}, u32[]{:S(2)}) %collective-permute-start.1) | collective-permute-done | bytes 393248 | tf_op jit(solution)/shard_map/ppermute | solution.py:16
  65.5 8.0 %collective-permute-done.2 = bf16[2,1,1,128,768]{4,3,2,1,0:T(8,128)(2,1)} collective-permute-done((bf16[2,1,1,128,768]{4,3,2,1,0:T(8,128)(2,1)S(1)}, bf16[2,1,1,128,768]{4,3,2,1,0:T(8,128)(2,1)}, u32[]{:S(2)}, u32[]{:S(2)}) %collective-permute-start.2) | collective-permute-done | bytes 393248 | tf_op jit(solution)/shard_map/ppermute | solution.py:16
  79.3 4.1 gather_fusion
  96.5 5.9 %fusion.28 = (f32[12,128]{1,0:T(8,128)S(1)}, f32[12,128,896]{1,2,0:T(8,128)}) fusion(pred[896]{0:T(1024)(128)(4,1)S(1)} %broadcast_bitcast_fusion, bf16[896,12,64]{0,2,1:T(8,128)(2,1)} %squeeze.37, bf16[128,12,64]{0,2,1:T(8,128)(2,1)S(1)} %bitcast.88), kind=kOutput, calls=%fused_computation.65 | convolution fusion | flops 181666688 | bytes 7084928 | tf_op jit(solution)/shard_map/while/body/eval_jaxpr/sub | solution.py:72
  102.4 3.3 fusion.8
  112.0 4.2 stack.25
  116.2 4.5 multiply_bitcast_fusion
  120.7 4.2 stack.24
  126.4 6.1 %maximum_bitcast_fusion = f32[7,2,128,768]{2,0,3,1:T(8,128)} fusion(f32[1,1,7,128,768]{3,2,4,1,0:T(8,128)} %stack.25, f32[1,1,7,128,768]{3,2,4,1,0:T(8,128)} %stack.24), kind=kLoop, calls=%fused_computation.3 | loop fusion | flops 1376256 | bytes 11010048 | tf_op jit(solution)/shard_map/while/body/eval_jaxpr/stack | solution.py:99
  132.5 6.4 %copy.44 = f32[7,2,128,768]{3,2,1,0:T(8,128)} copy(f32[7,2,128,768]{2,0,3,1:T(8,128)} %maximum_bitcast_fusion) | data formatting | bytes 11010048 | tf_op jit(solution)/shard_map/while/body/eval_jaxpr/stack | solution.py:99
  141.8 14.2 %scatter_fusion = f32[2,7,128,768]{3,2,1,0:T(8,128)} fusion(f32[2,7,128,768]{3,2,1,0:T(8,128)} %broadcast.96, s32[7]{0:T(128)S(1)} %fusion.23, f32[7,2,128,768]{3,2,1,0:T(8,128)} %copy.44), kind=kCustom, calls=%fused_computation.1 | custom fusion | flops 1376256 | bytes 16515100 | tf_op jit(solution)/shard_map/scatter-add | solution.py:114
  162.7 10.5 %collective-permute-start.10 = (bf16[2,1,1,128,768]{4,3,2,0,1:T(8,128)(2,1)}, bf16[2,1,1,128,768]{4,3,2,0,1:T(8,128)(2,1)S(1)}, u32[]{:S(2)}, u32[]{:S(2)}) collective-permute-start(bf16[2,1,1,128,768]{4,3,2,0,1:T(8,128)(2,1)} %get-tuple-element.49), channel_id=1, source_target_pairs={{0,2},{1,3},{2,4},{3,5},{4,6},{5,7},{6,8},{7,9},{8,10},{9,11},{10,... | collective-permute-start | bytes 1179656 | tf_op jit(solution)/shard_map/ppermute | solution.py:16
  175.6 6.7 %collective-permute-start.8 = (bf16[2,1,1,128,768]{4,3,2,0,1:T(8,128)(2,1)}, bf16[2,1,1,128,768]{4,3,2,0,1:T(8,128)(2,1)}, u32[]{:S(2)}, u32[]{:S(2)}) collective-permute-start(bf16[2,1,1,128,768]{4,3,2,0,1:T(8,128)(2,1)} %get-tuple-element.51), channel_id=1, source_target_pairs={{0,63},{1,0},{2,1},{3,2},{4,3},{5,4},{6,5},{7,6},{8,7},{9,8},{10,9... | collective-permute-start | bytes 1179656 | tf_op jit(solution)/shard_map/ppermute | solution.py:16
  184.5 11.3 %collective-permute-done.11 = bf16[2,1,1,128,768]{4,3,2,0,1:T(8,128)(2,1)S(1)} collective-permute-done((bf16[2,1,1,128,768]{4,3,2,0,1:T(8,128)(2,1)S(1)}, bf16[2,1,1,128,768]{4,3,2,0,1:T(8,128)(2,1)S(1)}, u32[]{:S(2)}, u32[]{:S(2)}) %collective-permute-start.11) | collective-permute-done | bytes 393248 | tf_op jit(solution)/shard_map/ppermute | solution.py:16
  200.2 9.9 %collective-permute-done.10 = bf16[2,1,1,128,768]{4,3,2,0,1:T(8,128)(2,1)S(1)} collective-permute-done((bf16[2,1,1,128,768]{4,3,2,0,1:T(8,128)(2,1)}, bf16[2,1,1,128,768]{4,3,2,0,1:T(8,128)(2,1)S(1)}, u32[]{:S(2)}, u32[]{:S(2)}) %collective-permute-start.10) | collective-permute-done | bytes 393248 | tf_op jit(solution)/shard_map/ppermute | solution.py:16
  210.1 9.8 %collective-permute-done.9 = bf16[2,1,1,128,768]{4,3,2,0,1:T(8,128)(2,1)S(1)} collective-permute-done((bf16[2,1,1,128,768]{4,3,2,0,1:T(8,128)(2,1)}, bf16[2,1,1,128,768]{4,3,2,0,1:T(8,128)(2,1)S(1)}, u32[]{:S(2)}, u32[]{:S(2)}) %collective-permute-start.9) | collective-permute-done | bytes 393248 | tf_op jit(solution)/shard_map/ppermute | solution.py:16
  220.0 8.0 %collective-permute-done.6 = bf16[2,1,1,128,768]{4,3,2,0,1:T(8,128)(2,1)} collective-permute-done((bf16[2,1,1,128,768]{4,3,2,0,1:T(8,128)(2,1)S(1)}, bf16[2,1,1,128,768]{4,3,2,0,1:T(8,128)(2,1)}, u32[]{:S(2)}, u32[]{:S(2)}) %collective-permute-start.6) | collective-permute-done | bytes 393248 | tf_op jit(solution)/shard_map/ppermute | solution.py:16
  230.5 284.0 %all-reduce.1 = f32[96,768]{1,0:T(8,128)S(1)} all-reduce(bf16[96,768]{1,0:T(8,128)(2,1)} %reduce-scatter.2.cloned.1.call-done), channel_id=1, replica_groups=mesh['dp'=8,'station'=64] {'station'}, use_global_device_ids=true, to_apply=%region_5.6 | all-reduce | flops 73728 | bytes 442368 | tf_op jit(solution)/shard_map/psum | solution.py:135
  (72 shorter events, 60.0 us)
Async XLA Ops:
  7.2 27.5 %copy-start = (bf16[768,768]{1,0:T(8,128)(2,1)S(1)}, bf16[768,768]{1,0:T(8,128)(2,1)}, u32[]{:S(2)}) copy-start(bf16[768,768]{1,0:T(8,128)(2,1)} %param.11) | copy-start | bytes 3538948
  7.2 30.0 %copy-start.7 = (bf16[1,1,128,768]{3,2,1,0:T(8,128)(2,1)S(1)}, bf16[1,1,128,768]{3,2,1,0:T(8,128)(2,1)}, u32[]{:S(2)}) copy-start(bf16[1,1,128,768]{3,2,1,0:T(8,128)(2,1)} %param.7) | copy-start | bytes 589828
  7.2 223.3 %reduce-scatter.2.cloned.1.call-start = ((), (), s32[]{:S(2)}) async-start(), calls=%async_computation.1 | async-start | bytes 1327104 | tf_op jit(solution)/shard_map/reduce_scatter | solution.py:127
  7.2 68.0 %copy-start.5 = (bf16[1,1,128,768]{3,2,1,0:T(8,128)(2,1)S(1)}, bf16[1,1,128,768]{3,2,1,0:T(8,128)(2,1)}, u32[]{:S(2)}) copy-start(bf16[1,1,128,768]{3,2,1,0:T(8,128)(2,1)} %param.9) | copy-start | bytes 589828
  7.2 68.0 %copy-start.6 = (bf16[1,1,128,768]{3,2,1,0:T(8,128)(2,1)S(1)}, bf16[1,1,128,768]{3,2,1,0:T(8,128)(2,1)}, u32[]{:S(2)}) copy-start(bf16[1,1,128,768]{3,2,1,0:T(8,128)(2,1)} %param.8) | copy-start | bytes 589828
  8.4 40.0 %collective-permute-start = (bf16[2,1,1,128,768]{4,3,2,1,0:T(8,128)(2,1)S(1)}, bf16[2,1,1,128,768]{4,3,2,1,0:T(8,128)(2,1)}, u32[]{:S(2)}, u32[]{:S(2)}) collective-permute-start(bf16[2,1,1,128,768]{4,3,2,1,0:T(8,128)(2,1)S(1)} %pad_maximum_fusion), channel_id=1, source_target_pairs={{0,3},{1,4},{2,5},{3,6},{4,7},{5,8},{6,9},{7,10},{8,11},{9,12},{10... | collective-permute-start | bytes 1179656 | tf_op jit(solution)/shard_map/ppermute | solution.py:16
  15.0 48.7 %collective-permute-start.1 = (bf16[2,1,1,128,768]{4,3,2,1,0:T(8,128)(2,1)S(1)}, bf16[2,1,1,128,768]{4,3,2,1,0:T(8,128)(2,1)}, u32[]{:S(2)}, u32[]{:S(2)}) collective-permute-start(bf16[2,1,1,128,768]{4,3,2,1,0:T(8,128)(2,1)S(1)} %pad_maximum_fusion), channel_id=1, source_target_pairs={{0,2},{1,3},{2,4},{3,5},{4,6},{5,7},{6,8},{7,9},{8,10},{9,11},{10,... | collective-permute-start | bytes 1179656 | tf_op jit(solution)/shard_map/ppermute | solution.py:16
  21.4 52.1 %collective-permute-start.2 = (bf16[2,1,1,128,768]{4,3,2,1,0:T(8,128)(2,1)S(1)}, bf16[2,1,1,128,768]{4,3,2,1,0:T(8,128)(2,1)}, u32[]{:S(2)}, u32[]{:S(2)}) collective-permute-start(bf16[2,1,1,128,768]{4,3,2,1,0:T(8,128)(2,1)S(1)} %pad_maximum_fusion), channel_id=1, source_target_pairs={{0,1},{1,2},{2,3},{3,4},{4,5},{5,6},{6,7},{7,8},{8,9},{9,10},{10,1... | collective-permute-start | bytes 1179656 | tf_op jit(solution)/shard_map/ppermute | solution.py:16
  25.2 50.8 %collective-permute-start.3 = (bf16[2,1,1,128,768]{4,3,2,1,0:T(8,128)(2,1)S(1)}, bf16[2,1,1,128,768]{4,3,2,1,0:T(8,128)(2,1)S(1)}, u32[]{:S(2)}, u32[]{:S(2)}) collective-permute-start(bf16[2,1,1,128,768]{4,3,2,1,0:T(8,128)(2,1)S(1)} %pad_maximum_fusion), channel_id=1, source_target_pairs={{0,63},{1,0},{2,1},{3,2},{4,3},{5,4},{6,5},{7,6},{8,7},{9,8},{10,9... | collective-permute-start | bytes 1179656 | tf_op jit(solution)/shard_map/ppermute | solution.py:16
  30.6 46.3 %collective-permute-start.4 = (bf16[2,1,1,128,768]{4,3,2,1,0:T(8,128)(2,1)S(1)}, bf16[2,1,1,128,768]{4,3,2,1,0:T(8,128)(2,1)S(1)}, u32[]{:S(2)}, u32[]{:S(2)}) collective-permute-start(bf16[2,1,1,128,768]{4,3,2,1,0:T(8,128)(2,1)S(1)} %pad_maximum_fusion), channel_id=1, source_target_pairs={{0,62},{1,63},{2,0},{3,1},{4,2},{5,3},{6,4},{7,5},{8,6},{9,7},{10,... | collective-permute-start | bytes 1179656 | tf_op jit(solution)/shard_map/ppermute | solution.py:16
  48.4 30.1 %collective-permute-start.5 = (bf16[2,1,1,128,768]{4,3,2,1,0:T(8,128)(2,1)S(1)}, bf16[2,1,1,128,768]{4,3,2,1,0:T(8,128)(2,1)S(1)}, u32[]{:S(2)}, u32[]{:S(2)}) collective-permute-start(bf16[2,1,1,128,768]{4,3,2,1,0:T(8,128)(2,1)S(1)} %pad_maximum_fusion), channel_id=1, source_target_pairs={{0,61},{1,62},{2,63},{3,0},{4,1},{5,2},{6,3},{7,4},{8,5},{9,6},{10... | collective-permute-start | bytes 1179656 | tf_op jit(solution)/shard_map/ppermute | solution.py:16
  102.4 6.7 %slice-start = ((s8[5505024]{0:T(1024)(128)(4,1)}), s8[4194304]{0:T(1024)(128)(4,1)S(1)}, s32[]{:S(2)}) async-start(s8[5505024]{0:T(1024)(128)(4,1)} %bitcast.81), calls=%async_computation.2 | async-start | bytes 8388608
  105.7 2.7 copy-start.3
  105.7 3.4 slice-start.1
  120.7 4.2 copy-start.4
  158.9 38.7 %copy-start.1 = (bf16[12,128,896]{1,2,0:T(8,128)(2,1)S(1)}, bf16[12,128,896]{1,2,0:T(8,128)(2,1)}, u32[]{:S(2)}) copy-start(bf16[12,128,896]{1,2,0:T(8,128)(2,1)} %multiply_convert_fusion) | copy-start | bytes 8257540
  158.9 38.7 %copy-start.2 = (bf16[896,12,64]{0,2,1:T(8,128)(2,1)S(1)}, bf16[896,12,64]{0,2,1:T(8,128)(2,1)}, u32[]{:S(2)}) copy-start(bf16[896,12,64]{0,2,1:T(8,128)(2,1)} %squeeze.37) | copy-start | bytes 4128772
  160.0 35.7 %collective-permute-start.11 = (bf16[2,1,1,128,768]{4,3,2,0,1:T(8,128)(2,1)S(1)}, bf16[2,1,1,128,768]{4,3,2,0,1:T(8,128)(2,1)S(1)}, u32[]{:S(2)}, u32[]{:S(2)}) collective-permute-start(bf16[2,1,1,128,768]{4,3,2,0,1:T(8,128)(2,1)S(1)} %get-tuple-element.48), channel_id=1, source_target_pairs={{0,3},{1,4},{2,5},{3,6},{4,7},{5,8},{6,9},{7,10},{8,11},{9,12},{10... | collective-permute-start | bytes 1179656 | tf_op jit(solution)/shard_map/ppermute | solution.py:16
  162.7 47.4 %collective-permute-start.10 = (bf16[2,1,1,128,768]{4,3,2,0,1:T(8,128)(2,1)}, bf16[2,1,1,128,768]{4,3,2,0,1:T(8,128)(2,1)S(1)}, u32[]{:S(2)}, u32[]{:S(2)}) collective-permute-start(bf16[2,1,1,128,768]{4,3,2,0,1:T(8,128)(2,1)} %get-tuple-element.49), channel_id=1, source_target_pairs={{0,2},{1,3},{2,4},{3,5},{4,6},{5,7},{6,8},{7,9},{8,10},{9,11},{10,... | collective-permute-start | bytes 1179656 | tf_op jit(solution)/shard_map/ppermute | solution.py:16
  173.2 46.8 %collective-permute-start.9 = (bf16[2,1,1,128,768]{4,3,2,0,1:T(8,128)(2,1)}, bf16[2,1,1,128,768]{4,3,2,0,1:T(8,128)(2,1)S(1)}, u32[]{:S(2)}, u32[]{:S(2)}) collective-permute-start(bf16[2,1,1,128,768]{4,3,2,0,1:T(8,128)(2,1)} %get-tuple-element.50), channel_id=1, source_target_pairs={{0,1},{1,2},{2,3},{3,4},{4,5},{5,6},{6,7},{7,8},{8,9},{9,10},{10,1... | collective-permute-start | bytes 1179656 | tf_op jit(solution)/shard_map/ppermute | solution.py:16
  175.6 44.4 %collective-permute-start.8 = (bf16[2,1,1,128,768]{4,3,2,0,1:T(8,128)(2,1)}, bf16[2,1,1,128,768]{4,3,2,0,1:T(8,128)(2,1)}, u32[]{:S(2)}, u32[]{:S(2)}) collective-permute-start(bf16[2,1,1,128,768]{4,3,2,0,1:T(8,128)(2,1)} %get-tuple-element.51), channel_id=1, source_target_pairs={{0,63},{1,0},{2,1},{3,2},{4,3},{5,4},{6,5},{7,6},{8,7},{9,8},{10,9... | collective-permute-start | bytes 1179656 | tf_op jit(solution)/shard_map/ppermute | solution.py:16
  182.3 37.6 %collective-permute-start.7 = (bf16[2,1,1,128,768]{4,3,2,0,1:T(8,128)(2,1)S(1)}, bf16[2,1,1,128,768]{4,3,2,0,1:T(8,128)(2,1)}, u32[]{:S(2)}, u32[]{:S(2)}) collective-permute-start(bf16[2,1,1,128,768]{4,3,2,0,1:T(8,128)(2,1)S(1)} %get-tuple-element.52), channel_id=1, source_target_pairs={{0,62},{1,63},{2,0},{3,1},{4,2},{5,3},{6,4},{7,5},{8,6},{9,7},{10,... | collective-permute-start | bytes 1179656 | tf_op jit(solution)/shard_map/ppermute | solution.py:16
  195.7 32.2 %collective-permute-start.6 = (bf16[2,1,1,128,768]{4,3,2,0,1:T(8,128)(2,1)S(1)}, bf16[2,1,1,128,768]{4,3,2,0,1:T(8,128)(2,1)}, u32[]{:S(2)}, u32[]{:S(2)}) collective-permute-start(bf16[2,1,1,128,768]{4,3,2,0,1:T(8,128)(2,1)S(1)} %get-tuple-element.47), channel_id=1, source_target_pairs={{0,61},{1,62},{2,63},{3,0},{4,1},{5,2},{6,3},{7,4},{8,5},{9,6},{10... | collective-permute-start | bytes 1179656 | tf_op jit(solution)/shard_map/ppermute | solution.py:16
Sparse Core Ops, SparseCore 0:
  126.5 36.0 reduce-scatter.1
where the time goes:
time: 523 us; the launch traced here: 522 us
  blocking collectives  284 us (54%)
  waiting for transfers between devices  67.1 us (13%)
  starting transfers between devices  56.1 us (11%)
  local copies, waits for them, and re-layouts  44.7 us (9%)
  other arithmetic  34.6 us (7%)
  matrix products  21.4 us (4%)
  between operations  14.3 us (3%)
    psum x1, blocking collectives, local(): grad_weight = lax.psum(grad_weight, 'station')  284 us
    ppermute x12, waiting for transfers between devices, from_behind(): return lax.ppermute(value, axis, pairs)  67 us
    ppermute x12, starting transfers between devices, from_behind(): return lax.ppermute(value, axis, pairs)  56 us
    another operation x3, local copies, waits for them, and re-layouts, one_station(): jnp.stack([key_part, value_part], 0).reshape(2, -1, span_rows, model_width)  14.7 us
    scatter-add x1, other arithmetic, local(): spread = jnp.zeros((2, window_count, candidates, span_rows, model_width),...  14.2 us
  transfers between devices with their start and end apart: 13, of which 8 were waited for; matrix products, arithmetic and copies ran while one was open for 10% of the time, Pallas kernels for 0%

commit v1 on v0

--- a/solution.py
+++ b/solution.py
@@ -3,6 +3,7 @@
 import jax.numpy as jnp
 from jax import lax
 from jax.sharding import PartitionSpec as P
+from jax.lax import all_gather
 
 HEADS = 12
 PMAX = 6
@@ -132,7 +133,11 @@
         scatter_dimension=0,
         tiled=True,
     ).astype(jnp.float32)
-    grad_weight = lax.psum(grad_weight, "station")
+
+    def recast_the_pipes(w_in, bus_axis):
+        return jnp.sum(all_gather(w_in, axis_name=bus_axis), 0)
+
+    grad_weight = recast_the_pipes(grad_weight, bus_axis="station")
     grad_weight = grad_weight / math.sqrt(row_count * lax.axis_size("dp") * device_count)
     return (
         layer_output.reshape(query_states.shape),

time: 523 us -> 392 us (0.75)
  blocking collectives: 284 us -> 0 us
  waiting for transfers between devices: 67.1 us -> 205 us
  other arithmetic: 34.6 us -> 43.6 us
    psum x1 -> x0, blocking collectives: 284 us -> none  [local(): grad_weight = lax.psum(grad_weight, 'station')]
    all_gather x0 -> x1, waiting for transfers between devices: none -> 86.3 us  [recast_the_pipes(): return jnp.sum(all_gather(w_in, axis_name=bus_axis), 0)]
    reduce_scatter x1, waiting for transfers between devices: 0.01 us -> 36 us  [local(): lax.psum_scatter(lax.dot_general(mixed_flat, flat_grad, (((0,), (0,)), ((...]
    ppermute x12, waiting for transfers between devices: 67 us -> 82.9 us  [from_behind(): return lax.ppermute(value, axis, pairs)]
    reduce_sum x0 -> x1, other arithmetic: none -> 7.33 us  [recast_the_pipes(): return jnp.sum(all_gather(w_in, axis_name=bus_axis), 0)]
  transfers between devices with their start and end apart: 13 -> 14, of which waited for: 8 -> 10; matrix products, arithmetic and copies ran while one was open for 10% -> 18% of each run, Pallas kernels for 0% -> 0%
where the time goes in v1:
time: 392 us; the launch traced here: 390 us
  waiting for transfers between devices  205 us (52%)
  starting transfers between devices  57.1 us (15%)
  local copies, waits for them, and re-layouts  47.7 us (12%)
  other arithmetic  43.6 us (11%)
  matrix products  22.4 us (6%)
  between operations  14.3 us (4%)
    all_gather x1, waiting for transfers between devices, recast_the_pipes(): return jnp.sum(all_gather(w_in, axis_name=bus_axis), 0)  86.3 us
    ppermute x12, waiting for transfers between devices, from_behind(): return lax.ppermute(value, axis, pairs)  82.9 us
    ppermute x12, starting transfers between devices, from_behind(): return lax.ppermute(value, axis, pairs)  56.8 us
    reduce_scatter x1, waiting for transfers between devices, local(): lax.psum_scatter(lax.dot_general(mixed_flat, flat_grad, (((0,), (0,)), ((...  36 us
    another operation x3, local copies, waits for them, and re-layouts, one_station(): jnp.stack([key_part, value_part], 0).reshape(2, -1, span_rows, model_width)  14.6 us
    scatter-add x1, other arithmetic, local(): spread = jnp.zeros((2, window_count, candidates, span_rows, model_width),...  14.2 us
    unnamed x27, local copies, waits for them, and re-layouts  11 us
  transfers between devices with their start and end apart: 14, of which 10 were waited for; matrix products, arithmetic and copies ran while one was open for 18% of the time, Pallas kernels for 0%

profile of v1, /device:TPU:24, one launch (start us, length us, event | category | flops | bytes accessed | tf_op | source)
XLA Modules:
  0.0 390.4 jit_solution(12407170018343535910)
XLA Ops:
  8.4 6.5 %collective-permute-start = (bf16[2,1,1,128,768]{4,3,2,1,0:T(8,128)(2,1)S(1)}, bf16[2,1,1,128,768]{4,3,2,1,0:T(8,128)(2,1)}, u32[]{:S(2)}, u32[]{:S(2)}) collective-permute-start(bf16[2,1,1,128,768]{4,3,2,1,0:T(8,128)(2,1)S(1)} %pad_maximum_fusion), channel_id=1, source_target_pairs={{0,3},{1,4},{2,5},{3,6},{4,7},{5,8},{6,9},{7,10},{8,11},{9,12},{10... | collective-permute-start | bytes 1179656 | tf_op jit(solution)/shard_map/ppermute | solution.py:17
  15.0 6.4 %collective-permute-start.1 = (bf16[2,1,1,128,768]{4,3,2,1,0:T(8,128)(2,1)S(1)}, bf16[2,1,1,128,768]{4,3,2,1,0:T(8,128)(2,1)}, u32[]{:S(2)}, u32[]{:S(2)}) collective-permute-start(bf16[2,1,1,128,768]{4,3,2,1,0:T(8,128)(2,1)S(1)} %pad_maximum_fusion), channel_id=1, source_target_pairs={{0,2},{1,3},{2,4},{3,5},{4,6},{5,7},{6,8},{7,9},{8,10},{9,11},{10,... | collective-permute-start | bytes 1179656 | tf_op jit(solution)/shard_map/ppermute | solution.py:17
  25.2 5.3 %collective-permute-start.3 = (bf16[2,1,1,128,768]{4,3,2,1,0:T(8,128)(2,1)S(1)}, bf16[2,1,1,128,768]{4,3,2,1,0:T(8,128)(2,1)S(1)}, u32[]{:S(2)}, u32[]{:S(2)}) collective-permute-start(bf16[2,1,1,128,768]{4,3,2,1,0:T(8,128)(2,1)S(1)} %pad_maximum_fusion), channel_id=1, source_target_pairs={{0,63},{1,0},{2,1},{3,2},{4,3},{5,4},{6,5},{7,6},{8,7},{9,8},{10,9... | collective-permute-start | bytes 1179656 | tf_op jit(solution)/shard_map/ppermute | solution.py:17
  37.4 11.0 %collective-permute-done = bf16[2,1,1,128,768]{4,3,2,1,0:T(8,128)(2,1)} collective-permute-done((bf16[2,1,1,128,768]{4,3,2,1,0:T(8,128)(2,1)S(1)}, bf16[2,1,1,128,768]{4,3,2,1,0:T(8,128)(2,1)}, u32[]{:S(2)}, u32[]{:S(2)}) %collective-permute-start) | collective-permute-done | bytes 393248 | tf_op jit(solution)/shard_map/ppermute | solution.py:17
  48.4 5.5 %collective-permute-start.5 = (bf16[2,1,1,128,768]{4,3,2,1,0:T(8,128)(2,1)S(1)}, bf16[2,1,1,128,768]{4,3,2,1,0:T(8,128)(2,1)S(1)}, u32[]{:S(2)}, u32[]{:S(2)}) collective-permute-start(bf16[2,1,1,128,768]{4,3,2,1,0:T(8,128)(2,1)S(1)} %pad_maximum_fusion), channel_id=1, source_target_pairs={{0,61},{1,62},{2,63},{3,0},{4,1},{5,2},{6,3},{7,4},{8,5},{9,6},{10... | collective-permute-start | bytes 1179656 | tf_op jit(solution)/shard_map/ppermute | solution.py:17
  55.7 8.0 %collective-permute-done.1 = bf16[2,1,1,128,768]{4,3,2,1,0:T(8,128)(2,1)} collective-permute-done((bf16[2,1,1,128,768]{4,3,2,1,0:T(8,128)(2,1)S(1)}, bf16[2,1,1,128,768]{4,3,2,1,0:T(8,128)(2,1)}, u32[]{:S(2)}, u32[]{:S(2)}) %collective-permute-start.1) | collective-permute-done | bytes 393248 | tf_op jit(solution)/shard_map/ppermute | solution.py:17
  65.5 8.0 %collective-permute-done.2 = bf16[2,1,1,128,768]{4,3,2,1,0:T(8,128)(2,1)} collective-permute-done((bf16[2,1,1,128,768]{4,3,2,1,0:T(8,128)(2,1)S(1)}, bf16[2,1,1,128,768]{4,3,2,1,0:T(8,128)(2,1)}, u32[]{:S(2)}, u32[]{:S(2)}) %collective-permute-start.2) | collective-permute-done | bytes 393248 | tf_op jit(solution)/shard_map/ppermute | solution.py:17
  79.3 4.1 %gather_fusion = bf16[7,2,128,768]{3,2,1,0:T(8,128)(2,1)} fusion(bf16[2,7,128,768]{3,2,1,0:T(8,128)(2,1)} %bitcast.2, s32[1024]{0:T(1024)S(1)} %pad_clamp_fusion), kind=kCustom, calls=%fused_computation | custom fusion | bytes 5505052 | tf_op jit(solution)/shard_map/while/body/eval_jaxpr/jit(_take)/gather | solution.py:63
  96.5 5.9 %fusion.28 = (f32[12,128]{1,0:T(8,128)S(1)}, f32[12,128,896]{1,2,0:T(8,128)}) fusion(pred[896]{0:T(1024)(128)(4,1)S(1)} %broadcast_bitcast_fusion, bf16[896,12,64]{0,2,1:T(8,128)(2,1)} %squeeze.37, bf16[128,12,64]{0,2,1:T(8,128)(2,1)S(1)} %bitcast.88), kind=kOutput, calls=%fused_computation.65 | convolution fusion | flops 181666688 | bytes 7084928 | tf_op jit(solution)/shard_map/while/body/eval_jaxpr/sub | solution.py:73
  109.7 36.0 %reduce-scatter.2.cloned.1.call-done = bf16[96,768]{1,0:T(8,128)(2,1)} async-done(((bf16[768,768]{1,0:T(8,128)(2,1)}), bf16[96,768]{1,0:T(8,128)(2,1)}) %reduce-scatter.2.cloned.1.call-update) | async-done | bytes 147472 | tf_op jit(solution)/shard_map/reduce_scatter | solution.py:128
  147.4 4.6 %convolution_bitcast_fusion = f32[896,12,64]{0,2,1:T(8,128)} fusion(bf16[128,12,64]{0,2,1:T(8,128)(2,1)S(1)} %bitcast.84, bf16[12,128,896]{1,2,0:T(8,128)(2,1)} %copy-done.1), kind=kOutput, calls=%fused_computation.17 | convolution fusion | flops 176160768 | bytes 5701632 | tf_op jit(solution)/shard_map/while/body/eval_jaxpr/hqk,qhd->khd/dot_general | solution.py:96
  168.2 6.0 %maximum_bitcast_fusion = f32[7,2,128,768]{2,0,3,1:T(8,128)} fusion(f32[1,1,7,128,768]{3,2,4,1,0:T(8,128)} %stack.25, f32[1,1,7,128,768]{3,2,4,1,0:T(8,128)} %stack.24), kind=kLoop, calls=%fused_computation.3 | loop fusion | flops 1376256 | bytes 11010048 | tf_op jit(solution)/shard_map/while/body/eval_jaxpr/stack | solution.py:100
  174.3 6.4 %copy.44 = f32[7,2,128,768]{3,2,1,0:T(8,128)} copy(f32[7,2,128,768]{2,0,3,1:T(8,128)} %maximum_bitcast_fusion) | data formatting | bytes 11010048 | tf_op jit(solution)/shard_map/while/body/eval_jaxpr/stack | solution.py:100
  183.6 14.2 %scatter_fusion = f32[2,7,128,768]{3,2,1,0:T(8,128)} fusion(f32[2,7,128,768]{3,2,1,0:T(8,128)} %broadcast.96, s32[7]{0:T(128)S(1)} %fusion.23, f32[7,2,128,768]{3,2,1,0:T(8,128)} %copy.44), kind=kCustom, calls=%fused_computation.1 | custom fusion | flops 1376256 | bytes 16515100 | tf_op jit(solution)/shard_map/scatter-add | solution.py:115
  201.9 5.5 %collective-permute-start.11 = (bf16[2,1,1,128,768]{4,3,2,0,1:T(8,128)(2,1)S(1)}, bf16[2,1,1,128,768]{4,3,2,0,1:T(8,128)(2,1)S(1)}, u32[]{:S(2)}, u32[]{:S(2)}) collective-permute-start(bf16[2,1,1,128,768]{4,3,2,0,1:T(8,128)(2,1)S(1)} %get-tuple-element.48), channel_id=1, source_target_pairs={{0,3},{1,4},{2,5},{3,6},{4,7},{5,8},{6,9},{7,10},{8,11},{9,12},{10... | collective-permute-start | bytes 1179656 | tf_op jit(solution)/shard_map/ppermute | solution.py:17
  207.4 5.8 %collective-permute-start.10 = (bf16[2,1,1,128,768]{4,3,2,0,1:T(8,128)(2,1)}, bf16[2,1,1,128,768]{4,3,2,0,1:T(8,128)(2,1)S(1)}, u32[]{:S(2)}, u32[]{:S(2)}) collective-permute-start(bf16[2,1,1,128,768]{4,3,2,0,1:T(8,128)(2,1)} %get-tuple-element.49), channel_id=1, source_target_pairs={{0,2},{1,3},{2,4},{3,5},{4,6},{5,7},{6,8},{7,9},{8,10},{9,11},{10,... | collective-permute-start | bytes 1179656 | tf_op jit(solution)/shard_map/ppermute | solution.py:17
  216.6 5.8 %collective-permute-start.8 = (bf16[2,1,1,128,768]{4,3,2,0,1:T(8,128)(2,1)}, bf16[2,1,1,128,768]{4,3,2,0,1:T(8,128)(2,1)}, u32[]{:S(2)}, u32[]{:S(2)}) collective-permute-start(bf16[2,1,1,128,768]{4,3,2,0,1:T(8,128)(2,1)} %get-tuple-element.51), channel_id=1, source_target_pairs={{0,63},{1,0},{2,1},{3,2},{4,3},{5,4},{6,5},{7,6},{8,7},{9,8},{10,9... | collective-permute-start | bytes 1179656 | tf_op jit(solution)/shard_map/ppermute | solution.py:17
  224.3 17.2 %collective-permute-done.11 = bf16[2,1,1,128,768]{4,3,2,0,1:T(8,128)(2,1)S(1)} collective-permute-done((bf16[2,1,1,128,768]{4,3,2,0,1:T(8,128)(2,1)S(1)}, bf16[2,1,1,128,768]{4,3,2,0,1:T(8,128)(2,1)S(1)}, u32[]{:S(2)}, u32[]{:S(2)}) %collective-permute-start.11) | collective-permute-done | bytes 393248 | tf_op jit(solution)/shard_map/ppermute | solution.py:17
  241.6 4.7 %collective-permute-start.6 = (bf16[2,1,1,128,768]{4,3,2,0,1:T(8,128)(2,1)S(1)}, bf16[2,1,1,128,768]{4,3,2,0,1:T(8,128)(2,1)}, u32[]{:S(2)}, u32[]{:S(2)}) collective-permute-start(bf16[2,1,1,128,768]{4,3,2,0,1:T(8,128)(2,1)S(1)} %get-tuple-element.47), channel_id=1, source_target_pairs={{0,61},{1,62},{2,63},{3,0},{4,1},{5,2},{6,3},{7,4},{8,5},{9,6},{10... | collective-permute-start | bytes 1179656 | tf_op jit(solution)/shard_map/ppermute | solution.py:17
  248.8 6.9 %collective-permute-done.10 = bf16[2,1,1,128,768]{4,3,2,0,1:T(8,128)(2,1)S(1)} collective-permute-done((bf16[2,1,1,128,768]{4,3,2,0,1:T(8,128)(2,1)}, bf16[2,1,1,128,768]{4,3,2,0,1:T(8,128)(2,1)S(1)}, u32[]{:S(2)}, u32[]{:S(2)}) %collective-permute-start.10) | collective-permute-done | bytes 393248 | tf_op jit(solution)/shard_map/ppermute | solution.py:17
  255.7 20.2 %collective-permute-done.9 = bf16[2,1,1,128,768]{4,3,2,0,1:T(8,128)(2,1)S(1)} collective-permute-done((bf16[2,1,1,128,768]{4,3,2,0,1:T(8,128)(2,1)}, bf16[2,1,1,128,768]{4,3,2,0,1:T(8,128)(2,1)S(1)}, u32[]{:S(2)}, u32[]{:S(2)}) %collective-permute-start.9) | collective-permute-done | bytes 393248 | tf_op jit(solution)/shard_map/ppermute | solution.py:17
  275.9 10.6 %collective-permute-done.6 = bf16[2,1,1,128,768]{4,3,2,0,1:T(8,128)(2,1)} collective-permute-done((bf16[2,1,1,128,768]{4,3,2,0,1:T(8,128)(2,1)S(1)}, bf16[2,1,1,128,768]{4,3,2,0,1:T(8,128)(2,1)}, u32[]{:S(2)}, u32[]{:S(2)}) %collective-permute-start.6) | collective-permute-done | bytes 393248 | tf_op jit(solution)/shard_map/ppermute | solution.py:17
  289.1 86.3 %all-gather.3.cloned.1.call-done = f32[6144,768]{1,0:T(8,128)} async-done(((f32[96,768]{1,0:T(8,128)}), f32[6144,768]{1,0:T(8,128)}) %all-gather.3.cloned.1.call-update) | async-done | bytes 18874384 | tf_op jit(solution)/shard_map/all_gather | solution.py:138
  375.4 7.3 %reduce_sum.31 = f32[96,768]{1,0:T(8,128)S(1)} reduce(f32[64,96,768]{2,1,0:T(8,128)} %bitcast.82, f32[]{:T(128)} %constant.88.clone.1), dimensions={0}, to_apply=%region_5.6 | reduce | flops 4644864 | bytes 19169284 | tf_op jit(solution)/shard_map/reduce_sum | solution.py:138
  (75 shorter events, 77.4 us)
Async XLA Ops:
  7.2 27.5 %copy-start = (bf16[768,768]{1,0:T(8,128)(2,1)S(1)}, bf16[768,768]{1,0:T(8,128)(2,1)}, u32[]{:S(2)}) copy-start(bf16[768,768]{1,0:T(8,128)(2,1)} %param.11) | copy-start | bytes 3538948
  7.2 30.0 %copy-start.9 = (bf16[1,1,128,768]{3,2,1,0:T(8,128)(2,1)S(1)}, bf16[1,1,128,768]{3,2,1,0:T(8,128)(2,1)}, u32[]{:S(2)}) copy-start(bf16[1,1,128,768]{3,2,1,0:T(8,128)(2,1)} %param.7) | copy-start | bytes 589828
  7.2 138.5 %reduce-scatter.2.cloned.1.call-start = ((), (), s32[]{:S(2)}) async-start(), calls=%async_computation.1 | async-start | bytes 1327104 | tf_op jit(solution)/shard_map/reduce_scatter | solution.py:128
  7.2 68.0 %copy-start.7 = (bf16[1,1,128,768]{3,2,1,0:T(8,128)(2,1)S(1)}, bf16[1,1,128,768]{3,2,1,0:T(8,128)(2,1)}, u32[]{:S(2)}) copy-start(bf16[1,1,128,768]{3,2,1,0:T(8,128)(2,1)} %param.9) | copy-start | bytes 589828
  7.2 68.0 %copy-start.8 = (bf16[1,1,128,768]{3,2,1,0:T(8,128)(2,1)S(1)}, bf16[1,1,128,768]{3,2,1,0:T(8,128)(2,1)}, u32[]{:S(2)}) copy-start(bf16[1,1,128,768]{3,2,1,0:T(8,128)(2,1)} %param.8) | copy-start | bytes 589828
  8.4 40.0 %collective-permute-start = (bf16[2,1,1,128,768]{4,3,2,1,0:T(8,128)(2,1)S(1)}, bf16[2,1,1,128,768]{4,3,2,1,0:T(8,128)(2,1)}, u32[]{:S(2)}, u32[]{:S(2)}) collective-permute-start(bf16[2,1,1,128,768]{4,3,2,1,0:T(8,128)(2,1)S(1)} %pad_maximum_fusion), channel_id=1, source_target_pairs={{0,3},{1,4},{2,5},{3,6},{4,7},{5,8},{6,9},{7,10},{8,11},{9,12},{10... | collective-permute-start | bytes 1179656 | tf_op jit(solution)/shard_map/ppermute | solution.py:17
  15.0 48.7 %collective-permute-start.1 = (bf16[2,1,1,128,768]{4,3,2,1,0:T(8,128)(2,1)S(1)}, bf16[2,1,1,128,768]{4,3,2,1,0:T(8,128)(2,1)}, u32[]{:S(2)}, u32[]{:S(2)}) collective-permute-start(bf16[2,1,1,128,768]{4,3,2,1,0:T(8,128)(2,1)S(1)} %pad_maximum_fusion), channel_id=1, source_target_pairs={{0,2},{1,3},{2,4},{3,5},{4,6},{5,7},{6,8},{7,9},{8,10},{9,11},{10,... | collective-permute-start | bytes 1179656 | tf_op jit(solution)/shard_map/ppermute | solution.py:17
  21.4 52.1 %collective-permute-start.2 = (bf16[2,1,1,128,768]{4,3,2,1,0:T(8,128)(2,1)S(1)}, bf16[2,1,1,128,768]{4,3,2,1,0:T(8,128)(2,1)}, u32[]{:S(2)}, u32[]{:S(2)}) collective-permute-start(bf16[2,1,1,128,768]{4,3,2,1,0:T(8,128)(2,1)S(1)} %pad_maximum_fusion), channel_id=1, source_target_pairs={{0,1},{1,2},{2,3},{3,4},{4,5},{5,6},{6,7},{7,8},{8,9},{9,10},{10,1... | collective-permute-start | bytes 1179656 | tf_op jit(solution)/shard_map/ppermute | solution.py:17
  25.2 50.8 %collective-permute-start.3 = (bf16[2,1,1,128,768]{4,3,2,1,0:T(8,128)(2,1)S(1)}, bf16[2,1,1,128,768]{4,3,2,1,0:T(8,128)(2,1)S(1)}, u32[]{:S(2)}, u32[]{:S(2)}) collective-permute-start(bf16[2,1,1,128,768]{4,3,2,1,0:T(8,128)(2,1)S(1)} %pad_maximum_fusion), channel_id=1, source_target_pairs={{0,63},{1,0},{2,1},{3,2},{4,3},{5,4},{6,5},{7,6},{8,7},{9,8},{10,9... | collective-permute-start | bytes 1179656 | tf_op jit(solution)/shard_map/ppermute | solution.py:17
  30.6 46.3 %collective-permute-start.4 = (bf16[2,1,1,128,768]{4,3,2,1,0:T(8,128)(2,1)S(1)}, bf16[2,1,1,128,768]{4,3,2,1,0:T(8,128)(2,1)S(1)}, u32[]{:S(2)}, u32[]{:S(2)}) collective-permute-start(bf16[2,1,1,128,768]{4,3,2,1,0:T(8,128)(2,1)S(1)} %pad_maximum_fusion), channel_id=1, source_target_pairs={{0,62},{1,63},{2,0},{3,1},{4,2},{5,3},{6,4},{7,5},{8,6},{9,7},{10,... | collective-permute-start | bytes 1179656 | tf_op jit(solution)/shard_map/ppermute | solution.py:17
  48.4 30.1 %collective-permute-start.5 = (bf16[2,1,1,128,768]{4,3,2,1,0:T(8,128)(2,1)S(1)}, bf16[2,1,1,128,768]{4,3,2,1,0:T(8,128)(2,1)S(1)}, u32[]{:S(2)}, u32[]{:S(2)}) collective-permute-start(bf16[2,1,1,128,768]{4,3,2,1,0:T(8,128)(2,1)S(1)} %pad_maximum_fusion), channel_id=1, source_target_pairs={{0,61},{1,62},{2,63},{3,0},{4,1},{5,2},{6,3},{7,4},{8,5},{9,6},{10... | collective-permute-start | bytes 1179656 | tf_op jit(solution)/shard_map/ppermute | solution.py:17
  102.4 4.8 %copy-start.5 = (bf16[896,12,64]{0,2,1:T(8,128)(2,1)S(1)}, bf16[896,12,64]{0,2,1:T(8,128)(2,1)}, u32[]{:S(2)}) copy-start(bf16[896,12,64]{0,2,1:T(8,128)(2,1)} %squeeze.36) | copy-start | bytes 4128772
  105.6 1.6 copy-start.1
  105.6 2.3 copy-start.6
  109.4 266.0 %all-gather.3.cloned.1.call-start = ((), (), s32[]{:S(2)}) async-start(), calls=%async_computation.2 | async-start | bytes 19169280 | tf_op jit(solution)/shard_map/all_gather | solution.py:138
  159.9 1.5 copy-start.2
  200.8 45.5 %copy-start.3 = (bf16[12,128,896]{1,2,0:T(8,128)(2,1)S(1)}, bf16[12,128,896]{1,2,0:T(8,128)(2,1)}, u32[]{:S(2)}) copy-start(bf16[12,128,896]{1,2,0:T(8,128)(2,1)} %copy-done.2) | copy-start | bytes 8257540
  200.8 45.5 %copy-start.4 = (bf16[896,12,64]{0,2,1:T(8,128)(2,1)S(1)}, bf16[896,12,64]{0,2,1:T(8,128)(2,1)}, u32[]{:S(2)}) copy-start(bf16[896,12,64]{0,2,1:T(8,128)(2,1)} %squeeze.37) | copy-start | bytes 4128772
  201.9 39.7 %collective-permute-start.11 = (bf16[2,1,1,128,768]{4,3,2,0,1:T(8,128)(2,1)S(1)}, bf16[2,1,1,128,768]{4,3,2,0,1:T(8,128)(2,1)S(1)}, u32[]{:S(2)}, u32[]{:S(2)}) collective-permute-start(bf16[2,1,1,128,768]{4,3,2,0,1:T(8,128)(2,1)S(1)} %get-tuple-element.48), channel_id=1, source_target_pairs={{0,3},{1,4},{2,5},{3,6},{4,7},{5,8},{6,9},{7,10},{8,11},{9,12},{10... | collective-permute-start | bytes 1179656 | tf_op jit(solution)/shard_map/ppermute | solution.py:17
  207.4 48.3 %collective-permute-start.10 = (bf16[2,1,1,128,768]{4,3,2,0,1:T(8,128)(2,1)}, bf16[2,1,1,128,768]{4,3,2,0,1:T(8,128)(2,1)S(1)}, u32[]{:S(2)}, u32[]{:S(2)}) collective-permute-start(bf16[2,1,1,128,768]{4,3,2,0,1:T(8,128)(2,1)} %get-tuple-element.49), channel_id=1, source_target_pairs={{0,2},{1,3},{2,4},{3,5},{4,6},{5,7},{6,8},{7,9},{8,10},{9,11},{10,... | collective-permute-start | bytes 1179656 | tf_op jit(solution)/shard_map/ppermute | solution.py:17
  213.2 62.7 %collective-permute-start.9 = (bf16[2,1,1,128,768]{4,3,2,0,1:T(8,128)(2,1)}, bf16[2,1,1,128,768]{4,3,2,0,1:T(8,128)(2,1)S(1)}, u32[]{:S(2)}, u32[]{:S(2)}) collective-permute-start(bf16[2,1,1,128,768]{4,3,2,0,1:T(8,128)(2,1)} %get-tuple-element.50), channel_id=1, source_target_pairs={{0,1},{1,2},{2,3},{3,4},{4,5},{5,6},{6,7},{7,8},{8,9},{9,10},{10,1... | collective-permute-start | bytes 1179656 | tf_op jit(solution)/shard_map/ppermute | solution.py:17
  216.6 59.3 %collective-permute-start.8 = (bf16[2,1,1,128,768]{4,3,2,0,1:T(8,128)(2,1)}, bf16[2,1,1,128,768]{4,3,2,0,1:T(8,128)(2,1)}, u32[]{:S(2)}, u32[]{:S(2)}) collective-permute-start(bf16[2,1,1,128,768]{4,3,2,0,1:T(8,128)(2,1)} %get-tuple-element.51), channel_id=1, source_target_pairs={{0,63},{1,0},{2,1},{3,2},{4,3},{5,4},{6,5},{7,6},{8,7},{9,8},{10,9... | collective-permute-start | bytes 1179656 | tf_op jit(solution)/shard_map/ppermute | solution.py:17
  222.4 53.5 %collective-permute-start.7 = (bf16[2,1,1,128,768]{4,3,2,0,1:T(8,128)(2,1)S(1)}, bf16[2,1,1,128,768]{4,3,2,0,1:T(8,128)(2,1)}, u32[]{:S(2)}, u32[]{:S(2)}) collective-permute-start(bf16[2,1,1,128,768]{4,3,2,0,1:T(8,128)(2,1)S(1)} %get-tuple-element.52), channel_id=1, source_target_pairs={{0,62},{1,63},{2,0},{3,1},{4,2},{5,3},{6,4},{7,5},{8,6},{9,7},{10,... | collective-permute-start | bytes 1179656 | tf_op jit(solution)/shard_map/ppermute | solution.py:17
  241.6 45.0 %collective-permute-start.6 = (bf16[2,1,1,128,768]{4,3,2,0,1:T(8,128)(2,1)S(1)}, bf16[2,1,1,128,768]{4,3,2,0,1:T(8,128)(2,1)}, u32[]{:S(2)}, u32[]{:S(2)}) collective-permute-start(bf16[2,1,1,128,768]{4,3,2,0,1:T(8,128)(2,1)S(1)} %get-tuple-element.47), channel_id=1, source_target_pairs={{0,61},{1,62},{2,63},{3,0},{4,1},{5,2},{6,3},{7,4},{8,5},{9,6},{10... | collective-permute-start | bytes 1179656 | tf_op jit(solution)/shard_map/ppermute | solution.py:17
Sparse Core Ops, SparseCore 0:
  109.5 36.0 reduce-scatter.1
  149.2 226.1 all-gather.2
